TPU v7x, 128 devices: a whole 4x4x4 slice. The times are simulated.
128 devices in a mesh: view: 16 (over y, z), depth: 8 (over x, core).
Axes of the slice: x: 4, y: 4, z: 4, core: 2. Of those that a mesh axis runs over, the one named last changes fastest.
Arguments:
- features: bfloat16 [48, 1024, 32], P('view'), may hold values from -6 to 6
- view_lists: int32 [48, 10], P('view'), may hold values from 0 to 31
- requests: int32 [16, 16, 2], replicated, may hold values from 0 to 2
- warp_idx: int32 [48, 10, 64, 8, 128], P('view', None, None, 'depth'), may hold values from -682 to 1023
- conv_weight: bfloat16 [27, 8, 8], replicated, may hold values from -0.4375 to 0.4375
Outputs:
- regularized: bfloat16 [48, 8, 64, 8, 128], P('view', None, 'depth')
Inputs may be any that keep to these rules, and one draw needn't show every extreme that they name: `warp_idx`: A negative entry marks a sample that falls outside the source tile and is left out of the sum and the count.
All inputs are finite; a program needn't handle non-finite values.
Results may differ from a plain program's by a relative error of at most 0.0049.
Values may be sent and summed in bfloat16 or wider, within the bound.
No kernel may reach another device: no remote copies, remote signals or barrier semaphores. Data moves between devices by JAX's collectives and lax.ppermute only.
A program may use at most 128 MiB of HBM per device.

v0:
```python
import jax
import jax.numpy as jnp
from jax import lax
from jax.sharding import PartitionSpec as P


def padded_2(cells, sides, width):
    for axis, dim in sides:
        count = lax.axis_size(axis)
        ends = count - 1
        head = lax.slice_in_dim(cells, 0, width, axis=dim)
        tail = lax.slice_in_dim(cells, cells.shape[dim] - width, cells.shape[dim], axis=dim)
        cells = jnp.concatenate(
            [
                lax.ppermute(tail, axis, [(i, (i + 1) % count) for i in range(ends)]),
                cells,
                lax.ppermute(head, axis, [((i + 1) % count, i) for i in range(ends)]),
            ],
            axis=dim,
        )
    return cells


def mix_taps(padded, conv_weight, depth_out, rows_out, cols_out):
    summed = None
    for depth_tap in range(3):
        for row_tap in range(3):
            for col_tap in range(3):
                shifted = padded[
                    :,
                    :,
                    depth_tap : depth_tap + depth_out,
                    row_tap : row_tap + rows_out,
                    col_tap : col_tap + cols_out,
                ]
                kernel = conv_weight[9 * depth_tap + 3 * row_tap + col_tap]
                term = jnp.einsum(
                    "vgdhw,gk->vkdhw", shifted, kernel, preferred_element_type=jnp.float32
                )
                summed = term if summed is None else summed + term
    return summed


def on_device(features, view_lists, requests, warp_idx, conv_weight):
    view_here = lax.axis_index("view")
    depth_here = lax.axis_index("depth")
    depth_count = lax.axis_size("depth")
    local_views = features.shape[0]
    pixels = features.shape[1]
    channels = features.shape[2]
    sources = warp_idx.shape[1]
    planes = warp_idx.shape[2]
    row_count = warp_idx.shape[3]
    columns = warp_idx.shape[4]
    groups = conv_weight.shape[1]
    asked = requests.shape[2]
    tile_pool = lax.all_gather(features, "view", axis=0, tiled=True)
    owner_dev = view_lists // asked
    slot_index = view_lists % asked
    source_ids = owner_dev * local_views + requests[view_here, owner_dev, slot_index]
    flat_pool = tile_pool.reshape(-1, channels)
    own_pixels = row_count * columns
    own_rows = lax.dynamic_slice_in_dim(features, depth_here * own_pixels, own_pixels, 1)

    def one_view(item):
        own_tile, warp_rows, view_sources = item
        usable = (warp_rows >= 0).reshape(sources, planes, own_pixels)
        picks = view_sources[:, None, None, None] * pixels + jnp.maximum(warp_rows, 0)
        warped = jnp.take(flat_pool, picks.reshape(-1), axis=0)
        warped = warped.reshape(sources, planes, own_pixels, groups, channels // groups)
        own_groups = own_tile.reshape(own_pixels, groups, channels // groups)
        products = jnp.einsum(
            "sdpgk,pgk->sdpg", warped, own_groups, preferred_element_type=jnp.float32
        )
        masked = jnp.where(usable[..., None], products, jnp.float32(0.0))
        live_count = jnp.sum(usable.astype(jnp.float32), axis=0)
        corr = 0.5 * jnp.sum(masked, axis=0) / jnp.maximum(live_count, jnp.float32(1.0))[..., None]
        corr = jnp.transpose(corr, (2, 0, 1)).reshape(groups, planes, row_count, columns)
        return corr.astype(jnp.bfloat16)

    cost_rows = lax.map(one_view, (own_rows, warp_idx, source_ids))
    slab_planes = planes // depth_count
    slab = lax.all_to_all(cost_rows, "depth", split_axis=2, concat_axis=3, tiled=True)
    rimmed = padded_2(slab, (("depth", 2),), 1)
    rimmed = jnp.pad(rimmed, ((0, 0), (0, 0), (0, 0), (1, 1), (1, 1)))
    summed = mix_taps(rimmed, conv_weight, slab_planes, row_count * depth_count, columns)
    return summed.astype(jnp.bfloat16)


def solution(mesh):
    return jax.shard_map(
        on_device,
        mesh=mesh,
        in_specs=(
            P("view", None, None),
            P("view", None),
            P(),
            P("view", None, None, "depth", None),
            P(),
        ),
        out_specs=P("view", None, "depth", None, None),
        check_vma=False,
    )
```

profile of v0, /device:TPU:1, one launch (start us, length us, event | category | flops | bytes accessed | tf_op | source)
XLA Modules:
  0.0 1019.4 jit_solution(8187742426238221678)
XLA Ops:
  6.5 0.7 all-gather.2.cloned.1.call-update
  7.3 0.7 fusion.81
  8.1 0.9 gather_fusion.1
  9.1 0.8 constant_dynamic-slice_fusion.2
  9.9 50.2 %all-gather.2.cloned.1.call-done = bf16[48,1024,32]{1,2,0:T(8,128)(2,1)} async-done(((bf16[3,1024,32]{1,2,0:T(8,128)(2,1)}), bf16[48,1024,32]{1,2,0:T(8,128)(2,1)}) %all-gather.2.cloned.1.call-update) | async-done | bytes 3145744 | tf_op jit(solution)/shard_map/all_gather | solution.py:57
  60.1 11.0 %copy.343 = bf16[48,1024,32]{2,1,0:T(8,128)(2,1)} copy(bf16[48,1024,32]{1,2,0:T(8,128)(2,1)} %all-gather.2.cloned.1.call-done) | data formatting | bytes 6291456 | tf_op jit(solution)/shard_map/while | solution.py:81
  71.1 909.2 %while.10 = (s32[]{:T(128)}, bf16[3,8,64,1,128]{4,1,0,3,2:T(8,128)(2,1)}, s32[3,10,64,1,128]{4,2,1,3,0:T(8,128)S(1)}, bf16[3,128,32]{1,2,0:T(8,128)(2,1)S(1)}, s...) while((s32[]{:T(128)}, bf16[3,8,64,1,128]{4,1,0,3,2:T(8,128)(2,1)}, ...), condition=%wide.region_3.4_spmd, body=%wide.region_0.3_spmd.sunk | while | flops 12587020 | bytes 46916348 | solution.py:81
  71.2 0.2 compare_and_fusion.2
  71.4 0.5 compare_select_fusion.5
  72.0 278.2 %gather_fusion = bf16[81920,32]{1,0:T(8,128)(2,1)} fusion(bf16[49152,32]{1,0:T(8,128)(2,1)} %get-tuple-element.177, s32[81920]{0:T(1024)S(1)} %broadcast_clamp_fusion.2), kind=kCustom, calls=%fused_computation.clone.1 | custom fusion | bytes 10813440 | tf_op jit(solution)/shard_map/while/body/eval_jaxpr/jit(_take)/gather | solution.py:69
  350.2 17.3 %copy.427 = bf16[81920,32]{0,1:T(8,128)(2,1)} copy(bf16[81920,32]{1,0:T(8,128)(2,1)} %gather_fusion) | data formatting | bytes 10485760 | tf_op jit(solution)/shard_map/while/body/eval_jaxpr/jit(_take)/gather | solution.py:69
  367.5 3.7 copy.428
  371.2 1.6 multiply_reduce_fusion.2
  372.9 0.3 fusion.122
  373.5 0.8 copy_dynamic-update-slice_fusion.2
  374.2 0.2 compare_and_fusion.2
  374.5 0.5 compare_select_fusion.5
  375.0 278.2 %gather_fusion = bf16[81920,32]{1,0:T(8,128)(2,1)} fusion(bf16[49152,32]{1,0:T(8,128)(2,1)} %get-tuple-element.177, s32[81920]{0:T(1024)S(1)} %broadcast_clamp_fusion.2), kind=kCustom, calls=%fused_computation.clone.1 | custom fusion | bytes 10813440 | tf_op jit(solution)/shard_map/while/body/eval_jaxpr/jit(_take)/gather | solution.py:69
  653.2 17.3 %copy.427 = bf16[81920,32]{0,1:T(8,128)(2,1)} copy(bf16[81920,32]{1,0:T(8,128)(2,1)} %gather_fusion) | data formatting | bytes 10485760 | tf_op jit(solution)/shard_map/while/body/eval_jaxpr/jit(_take)/gather | solution.py:69
  670.5 3.7 copy.428
  674.3 1.6 multiply_reduce_fusion.2
  676.0 0.3 fusion.122
  676.5 0.8 copy_dynamic-update-slice_fusion.2
  677.6 0.5 compare_select_fusion.5
  678.1 278.2 %gather_fusion = bf16[81920,32]{1,0:T(8,128)(2,1)} fusion(bf16[49152,32]{1,0:T(8,128)(2,1)} %get-tuple-element.177, s32[81920]{0:T(1024)S(1)} %broadcast_clamp_fusion.2), kind=kCustom, calls=%fused_computation.clone.1 | custom fusion | bytes 10813440 | tf_op jit(solution)/shard_map/while/body/eval_jaxpr/jit(_take)/gather | solution.py:69
  956.3 17.3 %copy.427 = bf16[81920,32]{0,1:T(8,128)(2,1)} copy(bf16[81920,32]{1,0:T(8,128)(2,1)} %gather_fusion) | data formatting | bytes 10485760 | tf_op jit(solution)/shard_map/while/body/eval_jaxpr/jit(_take)/gather | solution.py:69
  973.6 3.7 copy.428
  977.4 1.6 multiply_reduce_fusion.2
  979.0 0.3 fusion.122
  979.6 0.8 copy_dynamic-update-slice_fusion.2
  980.3 5.5 all-to-all-start
  989.8 3.8 all-to-all-done
  993.7 3.3 collective-permute-start
  997.0 2.1 collective-permute-start.1
  999.1 0.3 fusion.97
  999.4 3.0 collective-permute-done.1
  1002.4 0.5 select_maximum_fusion
  1002.9 0.3 fusion.76
  1003.3 0.3 fusion.51
  1003.6 0.3 fusion.53
  1003.9 0.3 fusion.55
  1004.2 0.3 fusion.57
  1004.5 0.3 fusion.59
  1004.9 0.3 fusion.61
  1005.2 0.3 fusion.63
  1005.5 0.3 fusion.65
  1005.8 0.3 fusion.67
  1006.1 0.3 fusion.69
  1006.5 0.3 fusion.71
  1006.8 0.3 convolution_bitcast_fusion.5
  1007.1 0.3 convolution_bitcast_fusion.6
  1007.4 0.3 convolution_bitcast_fusion.7
  1007.7 0.3 convolution_bitcast_fusion.8
  1008.0 0.3 convolution_bitcast_fusion.3
  1008.4 0.3 convolution_bitcast_fusion.4
  1008.7 0.3 convolution_bitcast_fusion.1
  1009.0 0.3 convolution_add_fusion.3
  1009.3 0.3 convolution_add_fusion.2
  1009.7 0.3 convolution_add_fusion.1
  1010.0 0.7 fusion.31
  1010.6 0.4 fusion.13
  1011.0 0.3 fusion.18
  1011.4 0.3 fusion.32
  1011.7 0.8 copy.309
  (75 shorter events, 5.7 us)
Async XLA Ops:
  6.5 1.5 copy-start
  6.5 3.3 copy-start.4
  6.5 53.6 %all-gather.2.cloned.1.call-start = ((), (), s32[]{:S(2)}) async-start(), calls=%async_computation.1 | async-start | bytes 3342336 | tf_op jit(solution)/shard_map/all_gather | solution.py:57
  9.8 61.3 %copy-start.3 = (s32[3,10,64,1,128]{4,3,2,1,0:T(1,128)S(1)}, s32[3,10,64,1,128]{4,3,2,1,0:T(1,128)}, u32[]{:S(2)}) copy-start(s32[3,10,64,1,128]{4,3,2,1,0:T(1,128)} %param.10) | copy-start | bytes 2949124
  71.1 914.7 %copy-start.2 = (bf16[27,8,8]{0,2,1:T(8,128)(2,1)S(1)}, bf16[27,8,8]{0,2,1:T(8,128)(2,1)}, u32[]{:S(2)}) copy-start(bf16[27,8,8]{0,2,1:T(8,128)(2,1)} %param.11) | copy-start | bytes 10372
  980.3 13.2 %all-to-all-start = ((bf16[3,8,64,1,128]{4,1,0,3,2:T(8,128)(2,1)}), bf16[3,8,64,1,128]{4,1,0,3,2:T(8,128)(2,1)S(1)}, u32[]{:S(2)}, u32[]{:S(2)}) async-start(bf16[3,8,64,1,128]{4,1,0,3,2:T(8,128)(2,1)} %get-tuple-element.37), calls=%async_computation | async-start | bytes 786432 | tf_op jit(solution)/shard_map/all_to_all | solution.py:83
  993.7 5.7 collective-permute-start
  997.0 5.4 collective-permute-start.1
  1011.0 1.5 copy-start.1
Sparse Core Ops, SparseCore 0:
  9.5 50.5 all-gather.1
where the time goes:
time: 1020 us
  local copies, waits for them, and re-layouts  918 us (90%)
  waiting for transfers between devices  57.7 us (6%)
  between operations  13.7 us (1%)
  starting transfers between devices  10.9 us (1%)
    gather x6, local copies, waits for them, and re-layouts, one_view(): warped = jnp.take(flat_pool, picks.reshape(-1), axis=0)  887 us
    all_gather x1, waiting for transfers between devices, on_device(): tile_pool = lax.all_gather(features, 'view', axis=0, tiled=True)  50.2 us
  transfers between devices with their start and end apart: 4, of which 3 were waited for; matrix products, arithmetic and copies ran while one was open for 1% of the time, Pallas kernels for 0%

commit v1 on v0

--- a/solution.py
+++ b/solution.py
@@ -54,7 +54,9 @@
     columns = warp_idx.shape[4]
     groups = conv_weight.shape[1]
     asked = requests.shape[2]
-    tile_pool = lax.all_gather(features, "view", axis=0, tiled=True)
+    tile_pool = jnp.concatenate(
+        lax.all_to_all(jnp.stack([features] * lax.axis_size("view")), "view", 0, 0), axis=0
+    )
     owner_dev = view_lists // asked
     slot_index = view_lists % asked
     source_ids = owner_dev * local_views + requests[view_here, owner_dev, slot_index]

time: 1020 us -> 1010 us (level)
  between operations: 13.7 us -> 0.28 us
  waiting for transfers between devices: 57.7 us -> 45.2 us
  starting transfers between devices: 10.9 us -> 21.4 us
    all_gather x1 -> x0, waiting for transfers between devices: 50.2 us -> none  [on_device(): tile_pool = lax.all_gather(features, 'view', axis=0, tiled=True)]
    all_to_all x0 -> x1, waiting for transfers between devices: none -> 38.4 us  [on_device(): lax.all_to_all(jnp.stack([features] * lax.axis_size('view')), 'view', 0, 0)]
where the time goes in v1:
time: 1010 us
  local copies, waits for them, and re-layouts  918 us (91%)
  waiting for transfers between devices  45.2 us (4%)
  starting transfers between devices  21.4 us (2%)
  other arithmetic  15 us (1%)
    gather x6, local copies, waits for them, and re-layouts, one_view(): warped = jnp.take(flat_pool, picks.reshape(-1), axis=0)  886 us
    all_to_all x1, waiting for transfers between devices, on_device(): lax.all_to_all(jnp.stack([features] * lax.axis_size('view')), 'view', 0, 0)  38.4 us
  transfers between devices with their start and end apart: 4, of which 3 were waited for; matrix products, arithmetic and copies ran while one was open for 1% of the time, Pallas kernels for 0%

profile of v1, /device:TPU:1, one launch (start us, length us, event | category | flops | bytes accessed | tf_op | source)
XLA Modules:
  0.0 1009.3 jit_solution(6272334789385146489)
XLA Ops:
  0.0 3.0 stack.2
  3.0 8.7 all-to-all-start
  11.8 0.9 gather_fusion.1
  12.9 0.8 constant_dynamic-slice_fusion.2
  13.6 38.4 %all-to-all-done = bf16[16,3,1024,32]{2,3,1,0:T(8,128)(2,1)S(1)} async-done(((bf16[16,3,1024,32]{2,3,1,0:T(8,128)(2,1)}), bf16[16,3,1024,32]{2,3,1,0:T(8,128)(2,1)S(1)}, u32[]{:S(2)}, u32[]{:S(2)}) %all-to-all-start) | async-done | bytes 3145760 | tf_op jit(solution)/shard_map/all_to_all | solution.py:58
  52.1 8.6 copy.343
  60.6 914.7 %while.10 = (s32[]{:T(128)}, bf16[3,8,64,1,128]{4,1,0,3,2:T(8,128)(2,1)}, s32[3,10,64,1,128]{4,2,1,3,0:T(8,128)}, bf16[3,128,32]{1,2,0:T(8,128)(2,1)S(1)}, s32[3...) while((s32[]{:T(128)}, bf16[3,8,64,1,128]{4,1,0,3,2:T(8,128)(2,1)}, ...), condition=%wide.region_3.4_spmd, body=%wide.region_0.3_spmd.sunk | while | flops 12587020 | bytes 46916348 | solution.py:83
  60.6 1.2 compare_and_fusion.2
  61.9 0.5 compare_select_fusion.5
  62.4 278.1 %gather_fusion = bf16[81920,32]{1,0:T(8,128)(2,1)} fusion(bf16[49152,32]{1,0:T(8,128)(2,1)} %get-tuple-element.177, s32[81920]{0:T(1024)S(1)} %broadcast_clamp_fusion.2), kind=kCustom, calls=%fused_computation.clone.1 | custom fusion | bytes 10813440 | tf_op jit(solution)/shard_map/while/body/eval_jaxpr/jit(_take)/gather | solution.py:71
  340.5 17.3 %copy.427 = bf16[81920,32]{0,1:T(8,128)(2,1)} copy(bf16[81920,32]{1,0:T(8,128)(2,1)} %gather_fusion) | data formatting | bytes 10485760 | tf_op jit(solution)/shard_map/while/body/eval_jaxpr/jit(_take)/gather | solution.py:71
  357.8 3.7 copy.428
  361.6 1.6 multiply_reduce_fusion.2
  363.2 1.0 convert_reduce_fusion.2
  364.8 0.8 copy_dynamic-update-slice_fusion.2
  365.5 1.2 compare_and_fusion.2
  366.8 0.5 compare_select_fusion.5
  367.3 278.1 %gather_fusion = bf16[81920,32]{1,0:T(8,128)(2,1)} fusion(bf16[49152,32]{1,0:T(8,128)(2,1)} %get-tuple-element.177, s32[81920]{0:T(1024)S(1)} %broadcast_clamp_fusion.2), kind=kCustom, calls=%fused_computation.clone.1 | custom fusion | bytes 10813440 | tf_op jit(solution)/shard_map/while/body/eval_jaxpr/jit(_take)/gather | solution.py:71
  645.4 17.3 %copy.427 = bf16[81920,32]{0,1:T(8,128)(2,1)} copy(bf16[81920,32]{1,0:T(8,128)(2,1)} %gather_fusion) | data formatting | bytes 10485760 | tf_op jit(solution)/shard_map/while/body/eval_jaxpr/jit(_take)/gather | solution.py:71
  662.7 3.7 copy.428
  666.5 1.6 multiply_reduce_fusion.2
  668.1 1.0 convert_reduce_fusion.2
  669.7 0.8 copy_dynamic-update-slice_fusion.2
  670.4 1.2 compare_and_fusion.2
  671.7 0.5 compare_select_fusion.5
  672.2 278.1 %gather_fusion = bf16[81920,32]{1,0:T(8,128)(2,1)} fusion(bf16[49152,32]{1,0:T(8,128)(2,1)} %get-tuple-element.177, s32[81920]{0:T(1024)S(1)} %broadcast_clamp_fusion.2), kind=kCustom, calls=%fused_computation.clone.1 | custom fusion | bytes 10813440 | tf_op jit(solution)/shard_map/while/body/eval_jaxpr/jit(_take)/gather | solution.py:71
  950.3 17.3 %copy.427 = bf16[81920,32]{0,1:T(8,128)(2,1)} copy(bf16[81920,32]{1,0:T(8,128)(2,1)} %gather_fusion) | data formatting | bytes 10485760 | tf_op jit(solution)/shard_map/while/body/eval_jaxpr/jit(_take)/gather | solution.py:71
  967.6 3.7 copy.428
  971.4 1.6 multiply_reduce_fusion.2
  973.0 1.0 convert_reduce_fusion.2
  974.6 0.8 copy_dynamic-update-slice_fusion.2
  975.3 7.3 all-to-all-start.1
  986.5 3.8 all-to-all-done.1
  990.5 3.3 collective-permute-start
  993.8 2.1 collective-permute-start.1
  996.2 3.0 collective-permute-done.1
  999.2 0.5 select_maximum_fusion
  999.7 0.3 fusion.76
  1000.0 0.3 fusion.51
  1000.3 0.3 fusion.53
  1000.7 0.3 fusion.55
  1001.0 0.3 fusion.57
  1001.3 0.3 fusion.59
  1001.6 0.3 fusion.61
  1001.9 0.3 fusion.63
  1002.3 0.3 fusion.65
  1002.6 0.3 fusion.67
  1002.9 0.3 fusion.69
  1003.2 0.3 fusion.71
  1003.5 0.3 convolution_bitcast_fusion.5
  1003.9 0.3 convolution_bitcast_fusion.6
  1004.2 0.3 convolution_bitcast_fusion.7
  1004.5 0.3 convolution_bitcast_fusion.8
  1004.8 0.3 convolution_bitcast_fusion.3
  1005.1 0.3 convolution_bitcast_fusion.4
  1005.5 0.3 convolution_bitcast_fusion.1
  1005.8 0.3 convolution_add_fusion.3
  1006.1 0.3 convolution_add_fusion.2
  1006.4 0.3 convolution_add_fusion.1
  1006.7 0.7 fusion.31
  1007.4 0.4 fusion.13
  1007.8 0.3 fusion.18
  1008.1 0.3 fusion.32
  1008.5 0.8 copy.309
  (73 shorter events, 6.5 us)
Async XLA Ops:
  0.0 11.8 %copy-start = (s32[16,16,2]{1,2,0:T(2,128)S(1)}, s32[16,16,2]{1,2,0:T(2,128)}, u32[]{:S(2)}) copy-start(s32[16,16,2]{1,2,0:T(2,128)} %param.9) | copy-start | bytes 6148
  3.0 8.7 copy-start.3
  3.0 49.1 %all-to-all-start = ((bf16[16,3,1024,32]{2,3,1,0:T(8,128)(2,1)}), bf16[16,3,1024,32]{2,3,1,0:T(8,128)(2,1)S(1)}, u32[]{:S(2)}, u32[]{:S(2)}) async-start(bf16[16,3,1024,32]{2,3,1,0:T(8,128)(2,1)} %stack.2), calls=%async_computation | async-start | bytes 6291456 | tf_op jit(solution)/shard_map/all_to_all | solution.py:58
  60.6 922.0 %copy-start.2 = (bf16[27,8,8]{0,2,1:T(8,128)(2,1)S(1)}, bf16[27,8,8]{0,2,1:T(8,128)(2,1)}, u32[]{:S(2)}) copy-start(bf16[27,8,8]{0,2,1:T(8,128)(2,1)} %param.11) | copy-start | bytes 10372
  975.3 15.0 %all-to-all-start.1 = ((bf16[3,8,64,1,128]{4,1,0,3,2:T(8,128)(2,1)}), bf16[3,8,64,1,128]{4,1,0,3,2:T(8,128)(2,1)S(1)}, u32[]{:S(2)}, u32[]{:S(2)}) async-start(bf16[3,8,64,1,128]{4,1,0,3,2:T(8,128)(2,1)} %get-tuple-element.37), calls=%async_computation.1 | async-start | bytes 786432 | tf_op jit(solution)/shard_map/all_to_all | solution.py:85
  990.5 5.7 collective-permute-start
  993.8 5.4 collective-permute-start.1
  1007.8 1.5 copy-start.1
